TPU v7x, 32 devices: a whole 2x2x4 slice. The times are simulated.
32 devices in a mesh: groups: 2 (over y), hist: 4 (over z), head: 2 (over x), rep: 2 (over core).
Axes of the slice: x: 2, y: 2, z: 4, core: 2. Of those that a mesh axis runs over, the one named last changes fastest.
Arguments:
- item_feats: bfloat16 [4096, 4096], P(('groups', 'hist', 'rep')), parts along dimension 0, may hold values from -6 to 6
- adapter: bfloat16 [4096, 512], P('hist', 'head'), may hold values from -0.09375 to 0.09375
- hist_emb: bfloat16 [8192, 512], P(('groups', 'hist')), parts along dimension 0, may hold values from -6 to 6
- key_weight: bfloat16 [512, 512], P(None, 'head'), may hold values from -0.25 to 0.25
- value_weight: bfloat16 [512, 512], P(None, 'head'), may hold values from -0.25 to 0.25
- routes: int32 [4096, 1], P(('groups', 'hist', 'rep')), parts along dimension 0, may hold values from 0 to 3; in each aligned block of 256 rows (0 to 255, 256 to 511, ...) at most 128 rows name the same one
- cand_index: int32 [1024], P(('groups', 'hist', 'rep')), parts along dimension 0, may hold values from 0 to 255
- item_user: int32 [4096], P(('groups', 'hist', 'rep')), parts along dimension 0, may hold values from 0 to 255
- hist_user: int32 [8192], P(('groups', 'hist')), parts along dimension 0, may hold values from 0 to 255
Outputs:
- scored: bfloat16 [1024, 512], P(('groups', 'hist', 'rep'), 'head'), parts along dimension 0
There are 2 independent parts, one for each index of `groups`. A program takes and returns all parts, laid end to end along the dimension named above; an argument that names none is the same for every part. Nothing has to cross between parts.
Inputs may be any that keep to these rules, and one draw needn't show every extreme that they name: `routes`: in the rows of one device no owner is named more than 128 times; some owner is named exactly 128 times.
All inputs are finite; a program needn't handle non-finite values.
Results may differ from a plain program's by a relative error of at most 0.0081.
Values may be sent and summed in bfloat16 or wider, within the bound.
A program may use at most 64 MiB of HBM per device.

v0:
```python
import math

import jax
import jax.numpy as jnp
from jax import lax
from jax.sharding import PartitionSpec as P

HS = 64


def attend(query_block, user_block, key_rows, value_rows, key_users):
    row_count = query_block.shape[0]
    col_count = query_block.shape[1]
    heads_here = col_count // HS
    att_scale = float(HS) ** (-0.5)
    query_three = query_block.reshape(row_count, heads_here, HS)
    key_three = key_rows.reshape(-1, heads_here, HS)
    value_three = value_rows.reshape(-1, heads_here, HS)
    scores = (
        jnp.einsum("rhd,khd->hrk", query_three, key_three, preferred_element_type=jnp.float32)
        * att_scale
    )
    matching = user_block[:, None] == key_users[None, :]
    weights = jnp.where(matching[None], jax.nn.silu(scores), 0.0).astype(jnp.bfloat16)
    mixture = jnp.einsum("hrk,khd->rhd", weights, value_three, preferred_element_type=jnp.float32)
    counted = jnp.sum(matching.astype(jnp.float32), axis=1)
    inverse = 1.0 / jnp.maximum(counted, 1.0)
    return mixture.reshape(row_count, col_count) * inverse[:, None]


def dense_partial(queries, users, key_rows, value_rows, key_users):
    total_rows = queries.shape[0]
    col_count = queries.shape[1]
    block_size = math.gcd(total_rows, 512)
    blocked_queries = queries.reshape(total_rows // block_size, block_size, col_count)
    blocked_users = users.reshape(total_rows // block_size, block_size)

    def one_block(operands):
        return attend(operands[0], operands[1], key_rows, value_rows, key_users)

    return lax.map(one_block, (blocked_queries, blocked_users)).reshape(total_rows, col_count)


def body(
    item_feats,
    adapter,
    hist_emb,
    key_weight,
    value_weight,
    routes,
    cand_index,
    item_user,
    hist_user,
):
    owners = lax.axis_size("hist")
    item_count = item_feats.shape[0]
    col_count = adapter.shape[1]
    embedded = jnp.dot(
        item_feats,
        lax.all_gather(adapter, "hist", axis=0, tiled=True),
        preferred_element_type=jnp.float32,
    ).astype(jnp.bfloat16)
    capacity = 2 * item_count // owners
    owner_of = routes[:, 0]
    owner_hot = (owner_of[:, None] == jnp.arange(owners, dtype=jnp.int32)[None, :]).astype(
        jnp.int32
    )
    earlier = jnp.cumsum(owner_hot, axis=0) - owner_hot
    slot_of = jnp.sum(earlier * owner_hot, axis=1)
    position = owner_of * capacity + slot_of
    placing = (jnp.arange(owners * capacity, dtype=jnp.int32)[:, None] == position[None, :]).astype(
        jnp.bfloat16
    )
    outgoing = jnp.dot(placing, embedded, preferred_element_type=jnp.float32).astype(jnp.bfloat16)
    outgoing = outgoing.reshape(owners, capacity, col_count)
    shifted_user = (item_user + 1).astype(jnp.bfloat16)
    outgoing_user = (
        jnp.dot(placing, shifted_user, preferred_element_type=jnp.float32) - 1.0
    ).astype(jnp.bfloat16)
    outgoing_user = outgoing_user.reshape(owners, capacity)
    incoming, incoming_user = (
        lax.all_to_all(outgoing, "hist", split_axis=0, concat_axis=0, tiled=True),
        lax.all_to_all(outgoing_user, "hist", split_axis=0, concat_axis=0, tiled=True),
    )
    routed, routed_user = (
        lax.all_gather(incoming, "rep", axis=0, tiled=True),
        lax.all_gather(incoming_user, "rep", axis=0, tiled=True),
    )
    routed = routed.reshape(-1, col_count)
    routed_user = routed_user.reshape(-1)
    key_local = jnp.dot(hist_emb, key_weight, preferred_element_type=jnp.float32).astype(
        jnp.bfloat16
    )
    value_local = jnp.dot(hist_emb, value_weight, preferred_element_type=jnp.float32).astype(
        jnp.bfloat16
    )
    key_rows = jnp.concatenate([key_local, routed], axis=0)
    value_rows = jnp.concatenate([value_local, routed], axis=0)
    key_users = jnp.concatenate([hist_user.astype(jnp.bfloat16), routed_user], axis=0)
    own_queries = embedded[cand_index]
    own_users = item_user[cand_index].astype(jnp.bfloat16)
    gathered, gathered_users = (
        lax.all_gather(own_queries, "hist", axis=0, tiled=True),
        lax.all_gather(own_users, "hist", axis=0, tiled=True),
    )
    partial_value = dense_partial(gathered, gathered_users, key_rows, value_rows, key_users)
    attended = lax.psum_scatter(partial_value, "hist", scatter_dimension=0, tiled=True)
    gating = jax.nn.silu(own_queries.astype(jnp.float32))
    return (gating * attended).astype(jnp.bfloat16)


def solution(mesh):
    placed = (
        P(("groups", "hist", "rep"), None),
        P("hist", "head"),
        P(("groups", "hist"), None),
        P(None, "head"),
        P(None, "head"),
        P(("groups", "hist", "rep"), None),
        P(("groups", "hist", "rep")),
        P(("groups", "hist", "rep")),
        P(("groups", "hist")),
    )
    return jax.shard_map(
        body,
        mesh=mesh,
        in_specs=placed,
        out_specs=P(("groups", "hist", "rep"), "head"),
        check_vma=False,
    )
```

profile of v0, /device:TPU:0, one launch (start us, length us, event | category | flops | bytes accessed | tf_op | source)
XLA Modules:
  0.0 119.3 jit_solution(5111718014451120370)
XLA Ops:
  6.5 0.0 copy-start
  6.5 0.0 all-gather.4.cloned.1.call-start
  6.6 0.7 all-gather.4.cloned.1.call-update
  7.3 0.8 add_convert_fusion.1
  8.1 0.7 compare_convert_fusion
  8.7 1.2 %reduce-window.6 = s32[4,2,128]{2,1,0:T(2,128)S(1)} reduce-window(s32[4,2,128]{2,1,0:T(2,128)S(1)} %compare_convert_fusion, s32[]{:T(128)} %constant.17.clone.1), window={size=1x1x128 pad=0_0x0_0x127_0}, to_apply=%region_0.0 | reduce-window | flops 130048 | bytes 8196 | tf_op jit(solution)/shard_map/reduce-window
  10.0 0.1 slice.12
  10.0 0.1 copy.20
  10.2 0.1 copy.21
  10.3 0.1 add_bitcast_fusion
  10.3 0.7 fusion.14
  11.0 0.7 multiply_add_fusion
  11.7 0.2 fusion.4
  11.9 0.6 copy.23
  12.5 6.3 %all-to-all-start.1 = ((bf16[4,1,128]{2,1,0:T(2,128)(2,1)}), bf16[4,1,128]{2,1,0:T(2,128)(2,1)S(1)}, u32[]{:S(2)}, u32[]{:S(2)}) async-start(bf16[4,1,128]{2,1,0:T(2,128)(2,1)} %copy.23), calls=%async_computation.1 | async-start | bytes 4096 | tf_op jit(solution)/shard_map/all_to_all | solution.py:83
  18.9 0.7 compare_select_fusion
  19.5 2.7 %convolution_convert_fusion = bf16[1024,256]{0,1:T(8,128)(2,1)} fusion(bf16[1024,512]{1,0:T(8,128)(2,1)} %param.11, bf16[512,256]{1,0:T(8,128)(2,1)} %param.12), kind=kOutput, calls=%fused_computation.5 | convolution fusion | flops 268697600 | bytes 1835008 | tf_op jit(solution)/shard_map/dot_general | solution.py:91
  22.2 0.0 copy-done.2
  22.2 1.3 %convolution_convert_fusion.1 = bf16[1024,256]{0,1:T(8,128)(2,1)} fusion(bf16[1024,512]{1,0:T(8,128)(2,1)S(1)} %copy-done.2, bf16[512,256]{1,0:T(8,128)(2,1)S(1)} %copy-done.5), kind=kOutput, calls=%fused_computation.6 | convolution fusion | flops 268697600 | bytes 1835008 | tf_op jit(solution)/shard_map/dot_general | solution.py:94
  23.5 0.0 copy-done.6
  23.6 0.8 gather_fusion.1
  24.4 0.6 dynamic-slice.2
  25.5 0.2 dynamic-update-slice
  25.7 12.6 %all-reduce = bf16[256]{0:T(256)(128)(2,1)S(1)} all-reduce(bf16[256]{0:T(256)(128)(2,1)S(1)} %dynamic-update-slice), channel_id=1, replica_groups=mesh['groups'=2,'hist'=4,'head'=2,'rep'=2] {'hist'}, use_global_device_ids=true, to_apply=%add | all-reduce | flops 256 | bytes 1024
  38.4 0.0 all-to-all-done.1
  38.4 1.8 %all-gather = bf16[8,1,128]{2,1,0:T(2,128)(2,1)S(1)} all-gather(bf16[4,1,128]{2,1,0:T(2,128)(2,1)S(1)} %all-to-all-done.1), channel_id=2, replica_groups=mesh['groups'=2,'hist'=4,'head'=2,'rep'=2] {'rep'}, dimensions={0}, use_global_device_ids=true | all-gather | bytes 3072 | tf_op jit(solution)/shard_map/all_gather | solution.py:87
  40.2 0.4 convert_reduce_fusion
  40.6 17.1 %all-gather.4.cloned.1.call-done = bf16[4096,256]{1,0:T(8,128)(2,1)} async-done(((bf16[1024,256]{1,0:T(8,128)(2,1)}), bf16[4096,256]{1,0:T(8,128)(2,1)}) %all-gather.4.cloned.1.call-update) | async-done | bytes 2097168 | tf_op jit(solution)/shard_map/all_gather | solution.py:60
  57.7 2.3 %convolution_convert_fusion.3 = bf16[256,256]{1,0:T(8,128)(2,1)S(1)} fusion(bf16[256,4096]{1,0:T(8,128)(2,1)S(1)} %copy-done, bf16[4096,256]{1,0:T(8,128)(2,1)} %all-gather.4.cloned.1.call-done), kind=kOutput, calls=%fused_computation.10 | convolution fusion | flops 536936448 | bytes 4325376 | tf_op jit(solution)/shard_map/dot_general | solution.py:58
  60.0 0.9 convolution_convert_fusion.2
  60.9 3.4 %all-to-all-start = ((bf16[4,128,256]{2,1,0:T(8,128)(2,1)}), bf16[4,128,256]{2,1,0:T(8,128)(2,1)S(1)}, u32[]{:S(2)}, u32[]{:S(2)}) async-start(bf16[4,128,256]{2,1,0:T(8,128)(2,1)} %bitcast.5), calls=%async_computation | async-start | bytes 524288 | tf_op jit(solution)/shard_map/all_to_all | solution.py:82
  64.3 0.0 reduce-scatter.2.cloned.1.call-start
  64.4 1.1 broadcast_compare_fusion
  65.5 0.7 gather_fusion
  66.2 0.0 copy-start.3
  66.2 14.3 %all-gather.1 = bf16[256,256]{1,0:T(8,128)(2,1)S(1)} all-gather(bf16[64,256]{1,0:T(8,128)(2,1)S(1)} %gather_fusion), channel_id=3, replica_groups=mesh['groups'=2,'hist'=4,'head'=2,'rep'=2] {'hist'}, dimensions={0}, use_global_device_ids=true | all-gather | bytes 163840 | tf_op jit(solution)/shard_map/all_gather | solution.py:103
  80.5 0.8 copy.24
  81.3 0.0 all-to-all-done
  81.3 2.2 %all_gather.16 = bf16[8,128,256]{2,1,0:T(8,128)(2,1)S(1)} all-gather(bf16[4,128,256]{2,1,0:T(8,128)(2,1)S(1)} %all-to-all-done), channel_id=1, replica_groups=mesh['groups'=2,'hist'=4,'head'=2,'rep'=2] {'rep'}, dimensions={0}, use_global_device_ids=true | all-gather | bytes 786432 | tf_op jit(solution)/shard_map/all_gather | solution.py:86
  83.5 0.3 copy.22
  83.8 0.2 concatenate.18
  84.0 0.0 copy-start.4
  84.0 5.2 %fusion = f32[4,64,256]{2,1,0:T(8,128)S(1)} fusion(bf16[256,4,64]{0,2,1:T(8,128)(2,1)} %bitcast.47, pred[256,2048]{1,0:T(8,128)(4,1)} %broadcast_compare_fusion, bf16[1024,4,64]{0,2,1:T(8,128)(2,1)S(1)} %concatenate.18, bf16[1024,4,64]{0,2,1:T(8,128)(2,1)} %bitcast.45, bf16[1024,4,64]{0,2,1:T(8,128)(2,1)} %bitcast.44), kind=kOutput, calls=%fused_computation.4 | convolution fusion | flops 555745280 | bytes 2490368 | tf_op jit(solution)/shard_map/while/body/eval_jaxpr/hrk,khd->rhd/dot_general | solution.py:25
  89.3 0.1 copy.25
  89.4 0.8 broadcast_multiply_fusion
  90.2 0.0 reduce-scatter.2.cloned.1.call-update
  90.2 20.8 %reduce-scatter.2.cloned.1.call-done = f32[64,256]{1,0:T(8,128)} async-done(((f32[256,256]{1,0:T(8,128)}), f32[64,256]{1,0:T(8,128)}) %reduce-scatter.2.cloned.1.call-update) | async-done | bytes 65552 | tf_op jit(solution)/shard_map/reduce_scatter | solution.py:107
  111.0 1.5 %fusion.11 = bf16[64,256]{1,0:T(8,128)(2,1)} fusion(f32[64,256]{1,0:T(8,128)} %reduce-scatter.2.cloned.1.call-done, bf16[64,256]{1,0:T(8,128)(2,1)S(1)} %copy-done.4), kind=kLoop, calls=%fused_computation.25 | loop fusion | flops 114688 | bytes 131072 | tf_op jit(solution)/shard_map/convert_element_type | solution.py:109
  (22 shorter events, 0.1 us)
Async XLA Ops:
  6.5 51.1 %copy-start = (bf16[256,4096]{1,0:T(8,128)(2,1)S(1)}, bf16[256,4096]{1,0:T(8,128)(2,1)}, u32[]{:S(2)}) copy-start(bf16[256,4096]{1,0:T(8,128)(2,1)} %param.9) | copy-start | bytes 6291460
  6.5 17.0 %copy-start.1 = (s32[256]{0:T(256)S(1)}, s32[256]{0:T(256)}, u32[]{:S(2)}) copy-start(s32[256]{0:T(256)} %param.16) | copy-start | bytes 3076
  6.5 15.7 %copy-start.2 = (bf16[1024,512]{1,0:T(8,128)(2,1)S(1)}, bf16[1024,512]{1,0:T(8,128)(2,1)}, u32[]{:S(2)}) copy-start(bf16[1024,512]{1,0:T(8,128)(2,1)} %param.11) | copy-start | bytes 3145732
  6.5 15.7 %copy-start.5 = (bf16[512,256]{1,0:T(8,128)(2,1)S(1)}, bf16[512,256]{1,0:T(8,128)(2,1)}, u32[]{:S(2)}) copy-start(bf16[512,256]{1,0:T(8,128)(2,1)} %param.13) | copy-start | bytes 786436
  6.5 17.0 %copy-start.6 = (s32[1024]{0:T(1024)S(1)}, s32[1024]{0:T(1024)}, u32[]{:S(2)}) copy-start(s32[1024]{0:T(1024)} %param.17) | copy-start | bytes 12292
  6.5 51.1 %all-gather.4.cloned.1.call-start = ((), (), s32[]{:S(2)}) async-start(), calls=%async_computation.3 | async-start | bytes 2621440 | tf_op jit(solution)/shard_map/all_gather | solution.py:60
  12.5 25.8 %all-to-all-start.1 = ((bf16[4,1,128]{2,1,0:T(2,128)(2,1)}), bf16[4,1,128]{2,1,0:T(2,128)(2,1)S(1)}, u32[]{:S(2)}, u32[]{:S(2)}) async-start(bf16[4,1,128]{2,1,0:T(2,128)(2,1)} %copy.23), calls=%async_computation.1 | async-start | bytes 4096 | tf_op jit(solution)/shard_map/all_to_all | solution.py:83
  19.5 4.8 %copy-start.7 = (u32[32]{0:T(128)S(1)}, u32[32]{0:T(128)}, u32[]{:S(2)}) copy-start(u32[32]{0:T(128)} %constant.42) | copy-start | bytes 388
  60.9 20.4 %all-to-all-start = ((bf16[4,128,256]{2,1,0:T(8,128)(2,1)}), bf16[4,128,256]{2,1,0:T(8,128)(2,1)S(1)}, u32[]{:S(2)}, u32[]{:S(2)}) async-start(bf16[4,128,256]{2,1,0:T(8,128)(2,1)} %bitcast.5), calls=%async_computation | async-start | bytes 524288 | tf_op jit(solution)/shard_map/all_to_all | solution.py:82
  64.3 46.7 %reduce-scatter.2.cloned.1.call-start = ((), (), s32[]{:S(2)}) async-start(), calls=%async_computation.4 | async-start | bytes 327680 | tf_op jit(solution)/shard_map/reduce_scatter | solution.py:107
  66.2 15.1 %copy-start.3 = (bf16[64,256]{1,0:T(8,128)(2,1)}, bf16[64,256]{1,0:T(8,128)(2,1)S(1)}, u32[]{:S(2)}) copy-start(bf16[64,256]{1,0:T(8,128)(2,1)S(1)} %gather_fusion) | copy-start | bytes 98308
  84.0 27.0 %copy-start.4 = (bf16[64,256]{1,0:T(8,128)(2,1)S(1)}, bf16[64,256]{1,0:T(8,128)(2,1)}, u32[]{:S(2)}) copy-start(bf16[64,256]{1,0:T(8,128)(2,1)} %copy-done.3) | copy-start | bytes 98308
Sparse Core Ops, SparseCore 0:
  8.9 48.7 all-gather.3
  90.3 20.6 reduce-scatter.1
where the time goes:
time: 120 us; the launch traced here: 119 us
  waiting for transfers between devices  38.6 us (32%)
  blocking collectives  30.9 us (26%)
  between operations  14.1 us (12%)
  matrix products  12.7 us (11%)
  starting transfers between devices  9.83 us (8%)
  other arithmetic  8.64 us (7%)
  local copies, waits for them, and re-layouts  4.62 us (4%)
    reduce_scatter x1, waiting for transfers between devices, body(): lax.psum_scatter(partial_value, 'hist', scatter_dimension=0, tiled=True)  20.8 us
    all_gather x1, waiting for transfers between devices, body(): lax.all_gather(adapter, 'hist', axis=0, tiled=True)  17.1 us
    all_gather x1, blocking collectives, body(): lax.all_gather(own_queries, 'hist', axis=0, tiled=True)  14.3 us
    unnamed x1, blocking collectives  12.6 us
    all_to_all x1, starting transfers between devices, body(): lax.all_to_all(outgoing_user, 'hist', split_axis=0, concat_axis=0, tiled=...  6.35 us
    dot_general x1, matrix products, attend(): jnp.einsum('hrk,khd->rhd', weights, value_three, preferred_element_type=j...  5.22 us
    all_to_all x1, starting transfers between devices, body(): lax.all_to_all(outgoing, 'hist', split_axis=0, concat_axis=0, tiled=True)  3.4 us
    dot_general x1, matrix products, body(): jnp.dot(hist_emb, key_weight, preferred_element_type=jnp.float32)  2.69 us
  transfers between devices with their start and end apart: 4, of which 2 were waited for; matrix products, arithmetic and copies ran while one was open for 12% of the time, Pallas kernels for 0%

commit v1 on v0

v1 whole, which is shorter than its diff:
```python
import functools

import jax
import jax.numpy as jnp
from jax import lax
from jax.experimental import pallas as pl
from jax.experimental.pallas import tpu as pltpu
from jax.sharding import PartitionSpec as P

HS = 64
USERS = 256
MESH = pl.DeviceIdType.MESH
F32 = jnp.float32
BF16 = jnp.bfloat16
NT = (((1,), (1,)), ((), ()))


def up(value, step):
    return -(-value // step) * step


def each(low, high, step):
    if high - low <= 8:
        for index in range(low, high):
            step(index)
    else:
        lax.fori_loop(low, high, lambda index, carry: (step(index), carry)[1], 0)


def iota(shape, axis):
    return lax.broadcasted_iota(jnp.int32, shape, axis)


def kernel(
    n,
    feats_hbm,
    adapter_hbm,
    hist_hbm,
    wk_hbm,
    wv_hbm,
    routes_ref,
    cand_ref,
    iuser_ref,
    huser_ref,
    out_ref,
    feats,
    ad,
    hist,
    wk,
    wv,
    k_all,
    v_all,
    acc,
    q_all,
    part_out,
    part_in,
    own_part,
    meta,
    meta_par,
    tab_all,
    ent_user,
    ent_scale,
    w_scr,
    local,
    feat_sem,
    z_send,
    z_recv,
    y_send,
    y_recv,
    p_send,
    p_recv,
    pp_send,
    pp_recv,
    q_send,
    q_recv,
    o_send,
    o_recv,
    t_send,
    t_recv,
    pair_send,
    pair_recv,
):
    me = lax.axis_index("hist")
    g = lax.axis_index("groups")
    r = lax.axis_index("rep")
    og, orep = 1 - g, 1 - r
    sign = jnp.where(me < n // 2, 1, -1)

    def peer(d):
        return lax.rem(me + sign * d + n, n)

    items, block = feats.shape[1], feats.shape[2]
    cols = ad.shape[2]
    heads = cols // HS
    cands = q_all.shape[1]
    events = hist.shape[0]
    entries = k_all.shape[0]
    owners = up(n, 8)
    rows = block // 4

    def share(a, b):
        return pl.ds(pl.multiple_of((a * 2 + b) * rows, rows), rows)

    def remote(src, dst, send, recv, where):
        return pltpu.make_async_remote_copy(
            src_ref=src, dst_ref=dst, send_sem=send, recv_sem=recv, device_id=where, device_id_type=MESH
        )

    barrier = pltpu.get_barrier_semaphore()
    each(1, n, lambda d: pl.semaphore_signal(barrier, inc=1, device_id={"hist": peer(d)}, device_id_type=MESH))
    pl.semaphore_signal(barrier, inc=1, device_id={"rep": orep}, device_id_type=MESH)
    pl.semaphore_signal(barrier, inc=1, device_id={"groups": og}, device_id_type=MESH)

    own_ad = pltpu.make_async_copy(adapter_hbm, ad.at[me], local.at[0])
    own_hist = pltpu.make_async_copy(hist_hbm, hist, local.at[1])
    own_wk = pltpu.make_async_copy(wk_hbm, wk, local.at[2])
    own_wv = pltpu.make_async_copy(wv_hbm, wv, local.at[3])
    for copy in (own_hist, own_wk, own_wv, own_ad):
        copy.start()

    def feat_copy(s):
        return pltpu.make_async_copy(
            feats_hbm.at[:, pl.ds(pl.multiple_of(s * block, 128), block)], feats.at[s], feat_sem.at[s]
        )

    each(0, n, lambda s: feat_copy(s).start())
    pl.semaphore_wait(barrier, n + 1)

    def z_copy(to):
        return remote(
            adapter_hbm.at[share(g, r)], ad.at[me, share(g, r)], z_send.at[to], z_recv.at[me], {"hist": to}
        )

    each(1, n, lambda d: z_copy(peer(n - d)).start())

    route_row = routes_ref[...].astype(F32)
    user_row = iuser_ref[...].astype(F32)

    def hot(row, count):
        shape = (count, row.shape[1])
        return jnp.where(iota(shape, 0).astype(F32) == row, 1.0, 0.0)

    owner_hot = hot(route_row, owners)
    user_hot = hot(user_row, USERS).astype(BF16)
    counts = lax.dot_general(owner_hot.astype(BF16), user_hot, NT, preferred_element_type=F32)
    meta[0:owners, 0:USERS] = counts
    meta[owners : owners + 1, 0:items] = user_row
    meta[owners + 1 : owners + 2, 0:items] = route_row
    meta_copy = remote(meta, meta_par, pair_send.at[0], pair_recv.at[0], {"rep": orep})
    meta_copy.start()

    cand_hot_t = hot(cand_ref[...].astype(F32), items)
    cand_hot = cand_hot_t.T.astype(BF16)
    cand_user = jnp.dot(
        jnp.broadcast_to(user_row, (8, items)).astype(BF16), cand_hot_t.astype(BF16), preferred_element_type=F32
    )
    event_row = huser_ref[...].astype(F32)
    event_hot = hot(event_row, USERS).astype(BF16)
    mine = jnp.where(iota((owners, events), 0) == me, 1.0, 0.0)
    event_counts = lax.dot_general(mine.astype(BF16), event_hot, NT, preferred_element_type=F32)

    meta_copy.wait_recv()
    tab_all[me, 0:owners, 0:USERS] = counts + event_counts + meta_par[0:owners, 0:USERS]
    tab_all[me, owners : owners + 8, 0:cands] = cand_user

    def t_copy(to):
        return remote(tab_all.at[me], tab_all.at[me], t_send.at[to], t_recv.at[me], {"hist": to})

    each(1, n, lambda d: t_copy(peer(d)).start())

    own_hist.wait()
    own_wk.wait()
    own_wv.wait()
    step_rows = min(events, 512)
    for start in range(0, events, step_rows):
        part = hist[start : start + step_rows, :]
        k_all[start : start + step_rows, :] = jnp.dot(part, wk[...], preferred_element_type=F32).astype(BF16)
        v_all[start : start + step_rows, :] = jnp.dot(part, wv[...], preferred_element_type=F32).astype(BF16)

    each(0, n, lambda s: feat_copy(s).wait())
    own_ad.wait()
    acc[...] = jnp.dot(feats[me], ad[me], preferred_element_type=F32)

    def hop(src, a, b, sends, recvs, where):
        ref = ad.at[src, share(a, b)]
        return remote(ref, ref, sends.at[src], recvs.at[src], where)

    def first(d):
        src = peer(d)
        hop(src, g, r, z_send, z_recv, {"hist": src}).wait_recv()
        hop(src, g, r, y_send, y_recv, {"groups": og}).start()
        hop(src, g, r, p_send, p_recv, {"rep": orep}).start()

    each(1, n, first)

    each(1, n, lambda d: remote(
        tab_all.at[peer(d)], tab_all.at[peer(d)], t_send.at[peer(d)], t_recv.at[peer(d)], {"hist": peer(d)}
    ).wait_recv())
    table = lax.fori_loop(
        0, n, lambda s, t: t + tab_all[s, 0:owners, 0:USERS], jnp.zeros((owners, USERS), F32)
    )
    high = jnp.floor(table * (1.0 / 256.0))
    split = jnp.concatenate([high, table - 256.0 * high], axis=0).astype(BF16)

    def scale_of(users_hot, owners_hot):
        both = jnp.dot(split, users_hot, preferred_element_type=F32)
        found = 256.0 * both[0:owners] + both[owners:]
        return 1.0 / jnp.maximum(jnp.sum(found * owners_hot, axis=0, keepdims=True), 1.0)

    par_user = meta_par[owners : owners + 1, 0:items]
    par_route = meta_par[owners + 1 : owners + 2, 0:items]
    ent_user[:, 0:events] = jnp.broadcast_to(event_row, (8, events))
    ent_user[:, events : events + items] = jnp.broadcast_to(user_row, (8, items))
    ent_user[:, events + items :] = jnp.broadcast_to(par_user, (8, items))
    ent_scale[:, 0:events] = jnp.broadcast_to(scale_of(event_hot, mine), (8, events))
    ent_scale[:, events : events + items] = jnp.broadcast_to(scale_of(user_hot, owner_hot), (8, items))
    ent_scale[:, events + items :] = jnp.broadcast_to(
        scale_of(hot(par_user, USERS).astype(BF16), hot(par_route, owners)), (8, items)
    )

    def second(d):
        src = peer(d)
        hop(src, og, r, y_send, y_recv, {"groups": og}).wait_recv()
        hop(src, og, r, pp_send, pp_recv, {"rep": orep}).start()

    each(1, n, second)

    def third(d):
        src = peer(d)
        hop(src, g, orep, p_send, p_recv, {"rep": orep}).wait_recv()
        hop(src, og, orep, pp_send, pp_recv, {"rep": orep}).wait_recv()
        acc[...] += jnp.dot(feats[src], ad[src], preferred_element_type=F32)

    each(1, n, third)

    embedded = acc[...].astype(BF16)
    own_q = jnp.dot(cand_hot, embedded, preferred_element_type=F32)
    q_all[me] = own_q.astype(BF16)

    def q_copy(to):
        return remote(q_all.at[me], q_all.at[me], q_send.at[to], q_recv.at[me], {"hist": to})

    each(1, n, lambda d: q_copy(peer(n - d)).start())
    k_all[events : events + items, :] = embedded
    v_all[events : events + items, :] = embedded
    emb_copy = remote(
        k_all.at[pl.ds(events, items)],
        k_all.at[pl.ds(events + items, items)],
        pair_send.at[1],
        pair_recv.at[1],
        {"rep": orep},
    )
    emb_copy.start()

    head_of = iota((1, cols), 1) // HS
    eye = iota((cands, cands), 0) == iota((cands, cands), 1)
    width = math_block(entries)

    def user_column(p):
        row = tab_all[p, owners : owners + 1, 0:cands]
        return jnp.sum(jnp.where(eye, row, 0.0), axis=1, keepdims=True)

    def q_wait(p):
        remote(q_all.at[p], q_all.at[p], q_send.at[p], q_recv.at[p], {"hist": p}).wait_recv()

    def o_copy(to):
        return remote(part_out.at[to], part_in.at[me], o_send.at[to], o_recv.at[me], {"hist": to})

    def chunk(pa, pb, opening):
        if not opening:
            q_wait(pa)
        q_wait(pb)
        q = jnp.concatenate([q_all[pa], q_all[pb]], axis=0) * jnp.asarray(0.5 * HS**-0.5, BF16)
        ucol = jnp.concatenate([user_column(pa), user_column(pb)], axis=0)
        count = 2 * cands
        stacked = jnp.concatenate([jnp.where(head_of == h, q, jnp.zeros_like(q)) for h in range(heads)], axis=0)
        for start in range(0, entries, width):
            if opening and start + width > events + items and start <= events + items:
                emb_copy.wait_recv()
                v_all[events + items :, :] = k_all[events + items :, :]
            half = lax.dot_general(stacked, k_all[start : start + width, :], NT, preferred_element_type=F32)
            scale = jnp.where(
                ucol == ent_user[0:1, start : start + width], ent_scale[0:1, start : start + width], 0.0
            )
            weight = (half + half * jnp.tanh(half)).reshape(heads, count, width) * scale[None]
            w_scr[:, start : start + width] = weight.reshape(heads * count, width).astype(BF16)
        mixed = jnp.dot(w_scr[...], v_all[...], preferred_element_type=F32)
        total = mixed[0:count]
        for h in range(1, heads):
            total = jnp.where(head_of == h, mixed[h * count : (h + 1) * count], total)
        if opening:
            own_part[...] = total[0:cands]
        else:
            part_out[pa] = total[0:cands].astype(BF16)
            o_copy(pa).start()
        part_out[pb] = total[cands:].astype(BF16)
        o_copy(pb).start()

    chunk(me, peer(1), True)
    each(1, n // 2, lambda c: chunk(peer(2 * c), peer(2 * c + 1), False))

    def collect(d):
        src = peer(d)
        remote(part_out.at[src], part_in.at[src], o_send.at[src], o_recv.at[src], {"hist": src}).wait_recv()
        own_part[...] += part_in[src].astype(F32)

    each(1, n, collect)
    gate = own_q * (0.5 + 0.5 * jnp.tanh(0.5 * own_q))
    out_ref[...] = (gate * own_part[...]).astype(BF16)

    def drain(d):
        p = peer(d)
        z_copy(p).wait_send()
        hop(p, g, r, y_send, y_recv, {"groups": og}).wait_send()
        hop(p, g, r, p_send, p_recv, {"rep": orep}).wait_send()
        hop(p, og, r, pp_send, pp_recv, {"rep": orep}).wait_send()
        t_copy(p).wait_send()
        q_copy(p).wait_send()
        o_copy(p).wait_send()

    each(1, n, drain)
    meta_copy.wait_send()
    emb_copy.wait_send()


def math_block(entries):
    return 256 if entries % 256 == 0 else 128


def body(item_feats, adapter, hist_emb, key_weight, value_weight, routes, cand_index, item_user, hist_user):
    n = lax.axis_size("hist")
    items, depth = item_feats.shape
    block, cols = adapter.shape
    events, dim = hist_emb.shape
    cands = cand_index.shape[0]
    heads = cols // HS
    owners = up(n, 8)
    wide = up(max(USERS, items, cands), 128)
    entries = events + 2 * items
    anywhere = pl.BlockSpec(memory_space=pl.ANY)
    vmem = pl.BlockSpec(memory_space=pltpu.VMEM)
    dma = pltpu.SemaphoreType.DMA
    return pl.pallas_call(
        functools.partial(kernel, n),
        out_shape=jax.ShapeDtypeStruct((cands, cols), BF16),
        in_specs=[anywhere] * 5 + [vmem] * 4,
        out_specs=vmem,
        scratch_shapes=[
            pltpu.VMEM((n, items, block), BF16),
            pltpu.VMEM((n, block, cols), BF16),
            pltpu.VMEM((events, dim), BF16),
            pltpu.VMEM((dim, cols), BF16),
            pltpu.VMEM((dim, cols), BF16),
            pltpu.VMEM((entries, cols), BF16),
            pltpu.VMEM((entries, cols), BF16),
            pltpu.VMEM((items, cols), F32),
            pltpu.VMEM((n, cands, cols), BF16),
            pltpu.VMEM((n, cands, cols), BF16),
            pltpu.VMEM((n, cands, cols), BF16),
            pltpu.VMEM((cands, cols), F32),
            pltpu.VMEM((owners + 8, wide), F32),
            pltpu.VMEM((owners + 8, wide), F32),
            pltpu.VMEM((n, owners + 8, wide), F32),
            pltpu.VMEM((8, entries), F32),
            pltpu.VMEM((8, entries), F32),
            pltpu.VMEM((heads * 2 * cands, entries), BF16),
            dma((4,)),
            dma((n,)),
        ]
        + [dma((n,))] * 14
        + [dma((2,)), dma((2,))],
        compiler_params=pltpu.CompilerParams(
            collective_id=0, has_side_effects=True, vmem_limit_bytes=48 * 1024 * 1024
        ),
    )(
        item_feats,
        adapter,
        hist_emb,
        key_weight,
        value_weight,
        routes.reshape(1, items),
        cand_index.reshape(1, cands),
        item_user.reshape(1, items),
        hist_user.reshape(1, events),
    )


def solution(mesh):
    placed = (
        P(("groups", "hist", "rep"), None),
        P("hist", "head"),
        P(("groups", "hist"), None),
        P(None, "head"),
        P(None, "head"),
        P(("groups", "hist", "rep"), None),
        P(("groups", "hist", "rep")),
        P(("groups", "hist", "rep")),
        P(("groups", "hist")),
    )
    return jax.shard_map(
        body,
        mesh=mesh,
        in_specs=placed,
        out_specs=P(("groups", "hist", "rep"), "head"),
        check_vma=False,
    )
```

time: 120 us -> 50.8 us (0.42)
  Pallas kernels: 0 us -> 41.3 us
  waiting for transfers between devices: 38.6 us -> 0 us
  blocking collectives: 30.9 us -> 0 us
  between operations: 14.1 us -> 0.02 us
  matrix products: 12.7 us -> 0 us
  starting transfers between devices: 9.83 us -> 0 us
  other arithmetic: 8.64 us -> 0 us
  local copies, waits for them, and re-layouts: 4.62 us -> 9.07 us
    pallas_call x0 -> x1, Pallas kernels: none -> 41.3 us  [body(): pl.pallas_call(functools.partial(kernel, n), out_shape=jax.ShapeDtypeStru...]
    reduce_scatter x1 -> x0, waiting for transfers between devices: 20.8 us -> none  [body(): lax.psum_scatter(partial_value, 'hist', scatter_dimension=0, tiled=True)]
    all_gather x3 -> x0, blocking collectives: 18.3 us -> none  [the longest x1 14.3 us: body(): lax.all_gather(own_queries, 'hist', axis=0, tiled=True)]
    all_gather x1 -> x0, waiting for transfers between devices: 17.1 us -> none  [body(): lax.all_gather(adapter, 'hist', axis=0, tiled=True)]
    dot_general x6 -> x0, matrix products: 12.7 us -> none  [the longest x1 5.22 us: attend(): jnp.einsum('hrk,khd->rhd', weights, value_three, preferred_element_type=j...]
    unnamed x1 -> x0, blocking collectives: 12.6 us -> none
    all_to_all x2 -> x0, starting transfers between devices: 9.75 us -> none  [the longest x1 6.35 us: body(): lax.all_to_all(outgoing_user, 'hist', split_axis=0, concat_axis=0, tiled=...]
    unnamed x19, local copies, waits for them, and re-layouts: 0.84 us -> 9.07 us
  transfers between devices with their start and end apart: 4 -> 0, of which waited for: 2 -> 0; matrix products, arithmetic and copies ran while one was open for 12% -> 0% of each run, Pallas kernels for 0% -> 0%
where the time goes in v1:
time: 50.8 us; the launch traced here: 50.4 us
  Pallas kernels  41.3 us (81%)
  local copies, waits for them, and re-layouts  9.07 us (18%)
    pallas_call x1, Pallas kernels, body(): pl.pallas_call(functools.partial(kernel, n), out_shape=jax.ShapeDtypeStru...  41.3 us
    unnamed x19, local copies, waits for them, and re-layouts  9.07 us

profile of v1, /device:TPU:0, one launch (start us, length us, event | category | flops | bytes accessed | tf_op | source)
XLA Modules:
  0.0 50.4 jit_solution(2246715260797993265)
XLA Ops:
  0.0 0.0 copy-start
  0.0 1.6 %copy-done = bf16[256,4096]{1,0:T(8,128)(2,1)S(1)} copy-done((bf16[256,4096]{1,0:T(8,128)(2,1)S(1)}, bf16[256,4096]{1,0:T(8,128)(2,1)}, u32[]{:S(2)}) %copy-start) | copy-done | bytes 2097176
  1.6 0.0 copy-start.1
  1.6 1.2 %copy-done.1 = bf16[1024,512]{1,0:T(8,128)(2,1)S(1)} copy-done((bf16[1024,512]{1,0:T(8,128)(2,1)S(1)}, bf16[1024,512]{1,0:T(8,128)(2,1)}, u32[]{:S(2)}) %copy-start.1) | copy-done | bytes 1048600
  2.8 0.0 copy-start.2
  2.8 1.0 %copy-done.2 = bf16[1024,256]{1,0:T(8,128)(2,1)S(1)} copy-done((bf16[1024,256]{1,0:T(8,128)(2,1)S(1)}, bf16[1024,256]{1,0:T(8,128)(2,1)}, u32[]{:S(2)}) %copy-start.2) | copy-done | bytes 524312
  3.9 0.0 copy-start.3
  3.9 0.9 %copy-done.3 = bf16[512,256]{1,0:T(8,128)(2,1)S(1)} copy-done((bf16[512,256]{1,0:T(8,128)(2,1)S(1)}, bf16[512,256]{1,0:T(8,128)(2,1)}, u32[]{:S(2)}) %copy-start.3) | copy-done | bytes 262168
  4.8 0.0 copy-start.4
  4.8 0.9 %copy-done.4 = bf16[512,256]{1,0:T(8,128)(2,1)S(1)} copy-done((bf16[512,256]{1,0:T(8,128)(2,1)S(1)}, bf16[512,256]{1,0:T(8,128)(2,1)}, u32[]{:S(2)}) %copy-start.4) | copy-done | bytes 262168
  5.8 0.0 copy-start.5
  5.8 0.7 %copy-done.5 = s32[1024]{0:T(1024)S(1)} copy-done((s32[1024]{0:T(1024)S(1)}, s32[1024]{0:T(1024)}, u32[]{:S(2)}) %copy-start.5) | copy-done | bytes 4120
  6.4 0.0 copy-start.6
  6.5 0.7 %copy-done.6 = s32[256,1]{0,1:T(1,128)S(1)} copy-done((s32[256,1]{0,1:T(1,128)S(1)}, s32[256,1]{0,1:T(1,128)}, u32[]{:S(2)}) %copy-start.6) | copy-done | bytes 1048
  7.1 0.0 copy-start.7
  7.1 0.7 %copy-done.7 = s32[256]{0:T(256)S(1)} copy-done((s32[256]{0:T(256)S(1)}, s32[256]{0:T(256)}, u32[]{:S(2)}) %copy-start.7) | copy-done | bytes 1048
  7.8 0.0 copy-start.8
  7.8 0.7 %copy-done.8 = s32[64]{0:T(128)S(1)} copy-done((s32[64]{0:T(128)S(1)}, s32[64]{0:T(128)}, u32[]{:S(2)}) %copy-start.8) | copy-done | bytes 280
  8.5 41.3 %shard_map.91 = bf16[64,256]{1,0:T(8,128)(2,1)S(1)} custom-call(bf16[256,4096]{1,0:T(8,128)(2,1)S(1)} %copy-done, bf16[1024,256]{1,0:T(8,128)(2,1)S(1)} %copy-done.2, bf16[1024,512]{1,0:T(8,128)(2,1)S(1)} %copy-done.1, bf16[512,256]{1,0:T(8,128)(2,1)S(1)} %copy-done.3, bf16[512,256]{1,0:T(8,128)(2,1)S(1)} %copy-done.4, s32[1,256]{1,0:T(1,128)S(1)} %bitcast.5, ...), custom_call_target="tpu_custom_call" | custom-call | tf_op jit(solution)/shard_map/pallas_call | solution.py:343
  49.8 0.6 %copy.11 = bf16[64,256]{1,0:T(8,128)(2,1)} copy(bf16[64,256]{1,0:T(8,128)(2,1)S(1)} %shard_map.91) | data formatting | bytes 65536
Async XLA Ops:
  0.0 1.6 %copy-start = (bf16[256,4096]{1,0:T(8,128)(2,1)S(1)}, bf16[256,4096]{1,0:T(8,128)(2,1)}, u32[]{:S(2)}) copy-start(bf16[256,4096]{1,0:T(8,128)(2,1)} %feats_hbm.1) | copy-start | bytes 6291460
  1.6 1.2 %copy-start.1 = (bf16[1024,512]{1,0:T(8,128)(2,1)S(1)}, bf16[1024,512]{1,0:T(8,128)(2,1)}, u32[]{:S(2)}) copy-start(bf16[1024,512]{1,0:T(8,128)(2,1)} %hist_hbm.1) | copy-start | bytes 3145732
  2.8 1.0 %copy-start.2 = (bf16[1024,256]{1,0:T(8,128)(2,1)S(1)}, bf16[1024,256]{1,0:T(8,128)(2,1)}, u32[]{:S(2)}) copy-start(bf16[1024,256]{1,0:T(8,128)(2,1)} %adapter_hbm.1) | copy-start | bytes 1572868
  3.9 0.9 %copy-start.3 = (bf16[512,256]{1,0:T(8,128)(2,1)S(1)}, bf16[512,256]{1,0:T(8,128)(2,1)}, u32[]{:S(2)}) copy-start(bf16[512,256]{1,0:T(8,128)(2,1)} %wk_hbm.1) | copy-start | bytes 786436
  4.8 0.9 %copy-start.4 = (bf16[512,256]{1,0:T(8,128)(2,1)S(1)}, bf16[512,256]{1,0:T(8,128)(2,1)}, u32[]{:S(2)}) copy-start(bf16[512,256]{1,0:T(8,128)(2,1)} %wv_hbm.1) | copy-start | bytes 786436
  5.8 0.7 %copy-start.5 = (s32[1024]{0:T(1024)S(1)}, s32[1024]{0:T(1024)}, u32[]{:S(2)}) copy-start(s32[1024]{0:T(1024)} %param.17) | copy-start | bytes 12292
  6.4 0.7 %copy-start.6 = (s32[256,1]{0,1:T(1,128)S(1)}, s32[256,1]{0,1:T(1,128)}, u32[]{:S(2)}) copy-start(s32[256,1]{0,1:T(1,128)} %param.14) | copy-start | bytes 3076
  7.1 0.7 %copy-start.7 = (s32[256]{0:T(256)S(1)}, s32[256]{0:T(256)}, u32[]{:S(2)}) copy-start(s32[256]{0:T(256)} %param.16) | copy-start | bytes 3076
  7.8 0.7 %copy-start.8 = (s32[64]{0:T(128)S(1)}, s32[64]{0:T(128)}, u32[]{:S(2)}) copy-start(s32[64]{0:T(128)} %param.15) | copy-start | bytes 772

commit v2 on v1

--- a/solution.py
+++ b/solution.py
@@ -8,6 +8,7 @@
 from jax.sharding import PartitionSpec as P
 
 HS = 64
+SUB = 2
 USERS = 256
 MESH = pl.DeviceIdType.MESH
 F32 = jnp.float32
@@ -38,11 +39,15 @@
     hist_hbm,
     wk_hbm,
     wv_hbm,
+    routes_hbm,
+    cand_hbm,
+    iuser_hbm,
+    huser_hbm,
+    out_ref,
     routes_ref,
     cand_ref,
     iuser_ref,
     huser_ref,
-    out_ref,
     feats,
     ad,
     hist,
@@ -63,7 +68,8 @@
     w_scr,
     local,
     feat_sem,
-    z_send,
+    left_send,
+    right_send,
     z_recv,
     y_send,
     y_recv,
@@ -96,10 +102,10 @@
     events = hist.shape[0]
     entries = k_all.shape[0]
     owners = up(n, 8)
-    rows = block // 4
-
-    def share(a, b):
-        return pl.ds(pl.multiple_of((a * 2 + b) * rows, rows), rows)
+    rows = block // (4 * SUB)
+
+    def share(a, b, k):
+        return pl.ds(pl.multiple_of(((a * 2 + b) * SUB + k) * rows, rows), rows)
 
     def remote(src, dst, send, recv, where):
         return pltpu.make_async_remote_copy(
@@ -115,7 +121,13 @@
     own_hist = pltpu.make_async_copy(hist_hbm, hist, local.at[1])
     own_wk = pltpu.make_async_copy(wk_hbm, wk, local.at[2])
     own_wv = pltpu.make_async_copy(wv_hbm, wv, local.at[3])
-    for copy in (own_hist, own_wk, own_wv, own_ad):
+    small = [
+        pltpu.make_async_copy(source, target, local.at[4 + place])
+        for place, (source, target) in enumerate(
+            ((routes_hbm, routes_ref), (iuser_hbm, iuser_ref), (cand_hbm, cand_ref), (huser_hbm, huser_ref))
+        )
+    ]
+    for copy in (*small, own_hist, own_wk, own_wv, own_ad):
         copy.start()
 
     def feat_copy(s):
@@ -126,13 +138,31 @@
     each(0, n, lambda s: feat_copy(s).start())
     pl.semaphore_wait(barrier, n + 1)
 
-    def z_copy(to):
+    def to_right(src, k, ref):
         return remote(
-            adapter_hbm.at[share(g, r)], ad.at[me, share(g, r)], z_send.at[to], z_recv.at[me], {"hist": to}
+            ref, ad.at[src, share(g, r, k)], right_send.at[src * SUB + k], z_recv.at[src * SUB + k], {"hist": me + 1}
         )
 
-    each(1, n, lambda d: z_copy(peer(n - d)).start())
-
+    def to_left(src, k, ref):
+        return remote(
+            ref, ad.at[src, share(g, r, k)], left_send.at[src * SUB + k], z_recv.at[src * SUB + k], {"hist": me - 1}
+        )
+
+    def piece(src, a, b, k):
+        return ad.at[src, share(a, b, k)]
+
+    for k in range(SUB):
+
+        @pl.when(me < n - 1)
+        def _():
+            to_right(me, k, adapter_hbm.at[share(g, r, k)]).start()
+
+        @pl.when(me > 0)
+        def _():
+            to_left(me, k, adapter_hbm.at[share(g, r, k)]).start()
+
+    for copy in small:
+        copy.wait()
     route_row = routes_ref[...].astype(F32)
     user_row = iuser_ref[...].astype(F32)
 
@@ -168,30 +198,76 @@
 
     each(1, n, lambda d: t_copy(peer(d)).start())
 
-    own_hist.wait()
-    own_wk.wait()
-    own_wv.wait()
-    step_rows = min(events, 512)
-    for start in range(0, events, step_rows):
-        part = hist[start : start + step_rows, :]
-        k_all[start : start + step_rows, :] = jnp.dot(part, wk[...], preferred_element_type=F32).astype(BF16)
-        v_all[start : start + step_rows, :] = jnp.dot(part, wv[...], preferred_element_type=F32).astype(BF16)
-
-    each(0, n, lambda s: feat_copy(s).wait())
-    own_ad.wait()
-    acc[...] = jnp.dot(feats[me], ad[me], preferred_element_type=F32)
-
-    def hop(src, a, b, sends, recvs, where):
-        ref = ad.at[src, share(a, b)]
-        return remote(ref, ref, sends.at[src], recvs.at[src], where)
-
-    def first(d):
-        src = peer(d)
-        hop(src, g, r, z_send, z_recv, {"hist": src}).wait_recv()
-        hop(src, g, r, y_send, y_recv, {"groups": og}).start()
-        hop(src, g, r, p_send, p_recv, {"rep": orep}).start()
-
-    each(1, n, first)
+    def hop(src, a, b, k, sends, recvs, where):
+        ref = piece(src, a, b, k)
+        return remote(ref, ref, sends.at[src * SUB + k], recvs.at[src * SUB + k], where)
+
+    def spread(src, k):
+        hop(src, g, r, k, y_send, y_recv, {"groups": og}).start()
+        hop(src, g, r, k, p_send, p_recv, {"rep": orep}).start()
+
+    def z_arrive(s):
+        for k in range(SUB):
+
+            @pl.when(me >= s)
+            def _():
+                src = me - s
+                ref = piece(src, g, r, k)
+                to_right(src, k, ref).wait_recv()
+
+                @pl.when(me < n - 1)
+                def _():
+                    to_right(src, k, ref).start()
+
+                spread(src, k)
+
+            @pl.when(me + s < n)
+            def _():
+                src = me + s
+                ref = piece(src, g, r, k)
+                to_left(src, k, ref).wait_recv()
+
+                @pl.when(me > 0)
+                def _():
+                    to_left(src, k, ref).start()
+
+                spread(src, k)
+
+    def y_pass(src):
+        for k in range(SUB):
+            hop(src, og, r, k, y_send, y_recv, {"groups": og}).wait_recv()
+            hop(src, og, r, k, pp_send, pp_recv, {"rep": orep}).start()
+
+    def y_arrive(s):
+        @pl.when(me >= s)
+        def _():
+            y_pass(me - s)
+
+        @pl.when(me + s < n)
+        def _():
+            y_pass(me + s)
+
+    def project():
+        own_hist.wait()
+        own_wk.wait()
+        own_wv.wait()
+        step_rows = min(events, 512)
+        for start in range(0, events, step_rows):
+            part = hist[start : start + step_rows, :]
+            k_all[start : start + step_rows, :] = jnp.dot(part, wk[...], preferred_element_type=F32).astype(BF16)
+            v_all[start : start + step_rows, :] = jnp.dot(part, wv[...], preferred_element_type=F32).astype(BF16)
+
+    def own_block():
+        each(0, n, lambda s: feat_copy(s).wait())
+        own_ad.wait()
+        acc[...] = jnp.dot(feats[me], ad[me], preferred_element_type=F32)
+
+    z_arrive(1)
+    project()
+    z_arrive(2)
+    y_arrive(1)
+    own_block()
+    each(3, n, lambda s: (z_arrive(s), y_arrive(s - 1)))
 
     each(1, n, lambda d: remote(
         tab_all.at[peer(d)], tab_all.at[peer(d)], t_send.at[peer(d)], t_recv.at[peer(d)], {"hist": peer(d)}
@@ -218,17 +294,13 @@
         scale_of(hot(par_user, USERS).astype(BF16), hot(par_route, owners)), (8, items)
     )
 
-    def second(d):
-        src = peer(d)
-        hop(src, og, r, y_send, y_recv, {"groups": og}).wait_recv()
-        hop(src, og, r, pp_send, pp_recv, {"rep": orep}).start()
-
-    each(1, n, second)
+    y_arrive(n - 1)
 
     def third(d):
         src = peer(d)
-        hop(src, g, orep, p_send, p_recv, {"rep": orep}).wait_recv()
-        hop(src, og, orep, pp_send, pp_recv, {"rep": orep}).wait_recv()
+        for k in range(SUB):
+            hop(src, g, orep, k, p_send, p_recv, {"rep": orep}).wait_recv()
+            hop(src, og, orep, k, pp_send, pp_recv, {"rep": orep}).wait_recv()
         acc[...] += jnp.dot(feats[src], ad[src], preferred_element_type=F32)
 
     each(1, n, third)
@@ -310,15 +382,29 @@
 
     def drain(d):
         p = peer(d)
-        z_copy(p).wait_send()
-        hop(p, g, r, y_send, y_recv, {"groups": og}).wait_send()
-        hop(p, g, r, p_send, p_recv, {"rep": orep}).wait_send()
-        hop(p, og, r, pp_send, pp_recv, {"rep": orep}).wait_send()
+        for k in range(SUB):
+            hop(p, g, r, k, y_send, y_recv, {"groups": og}).wait_send()
+            hop(p, g, r, k, p_send, p_recv, {"rep": orep}).wait_send()
+            hop(p, og, r, k, pp_send, pp_recv, {"rep": orep}).wait_send()
         t_copy(p).wait_send()
         q_copy(p).wait_send()
         o_copy(p).wait_send()
 
     each(1, n, drain)
+
+    def drain_right(s):
+        @pl.when((me >= s) & (me < n - 1))
+        def _():
+            for k in range(SUB):
+                to_right(me - s, k, piece(me - s, g, r, k)).wait_send()
+
+    def drain_left(s):
+        @pl.when((me + s < n) & (me > 0))
+        def _():
+            for k in range(SUB):
+                to_left(me + s, k, piece(me + s, g, r, k)).wait_send()
+
+    each(0, n, lambda s: (drain_right(s), drain_left(s)))
     meta_copy.wait_send()
     emb_copy.wait_send()
 
@@ -337,15 +423,19 @@
     owners = up(n, 8)
     wide = up(max(USERS, items, cands), 128)
     entries = events + 2 * items
-    anywhere = pl.BlockSpec(memory_space=pl.ANY)
+    hbm = pl.BlockSpec(memory_space=pltpu.HBM)
     vmem = pl.BlockSpec(memory_space=pltpu.VMEM)
     dma = pltpu.SemaphoreType.DMA
     return pl.pallas_call(
         functools.partial(kernel, n),
         out_shape=jax.ShapeDtypeStruct((cands, cols), BF16),
-        in_specs=[anywhere] * 5 + [vmem] * 4,
+        in_specs=[hbm] * 9,
         out_specs=vmem,
         scratch_shapes=[
+            pltpu.VMEM((1, items), jnp.int32),
+            pltpu.VMEM((1, cands), jnp.int32),
+            pltpu.VMEM((1, items), jnp.int32),
+            pltpu.VMEM((1, events), jnp.int32),
             pltpu.VMEM((n, items, block), BF16),
             pltpu.VMEM((n, block, cols), BF16),
             pltpu.VMEM((events, dim), BF16),
@@ -364,13 +454,14 @@
             pltpu.VMEM((8, entries), F32),
             pltpu.VMEM((8, entries), F32),
             pltpu.VMEM((heads * 2 * cands, entries), BF16),
-            dma((4,)),
+            dma((8,)),
             dma((n,)),
         ]
-        + [dma((n,))] * 14
+        + [dma((n * SUB,))] * 9
+        + [dma((n,))] * 6
         + [dma((2,)), dma((2,))],
         compiler_params=pltpu.CompilerParams(
-            collective_id=0, has_side_effects=True, vmem_limit_bytes=48 * 1024 * 1024
+            collective_id=0, has_side_effects=True
         ),
     )(
         item_feats,

time: 50.8 us -> 34.7 us (0.68)
  Pallas kernels: 41.3 us -> 33.2 us
  local copies, waits for them, and re-layouts: 9.07 us -> 1.38 us
    pallas_call x1, Pallas kernels: 41.3 us -> 33.2 us  [body(): pl.pallas_call(functools.partial(kernel, n), out_shape=jax.ShapeDtypeStru...]
    unnamed x19 -> x1, local copies, waits for them, and re-layouts: 9.07 us -> 1.38 us
where the time goes in v2:
time: 34.7 us; the launch traced here: 34.5 us
  Pallas kernels  33.2 us (96%)
  local copies, waits for them, and re-layouts  1.38 us (4%)
    pallas_call x1, Pallas kernels, body(): pl.pallas_call(functools.partial(kernel, n), out_shape=jax.ShapeDtypeStru...  33.2 us
    unnamed x1, local copies, waits for them, and re-layouts  1.38 us

profile of v2, /device:TPU:0, one launch (start us, length us, event | category | flops | bytes accessed | tf_op | source)
XLA Modules:
  0.0 34.5 jit_solution(17837937669988546229)
XLA Ops:
  0.0 33.2 %shard_map.91 = bf16[64,256]{1,0:T(8,128)(2,1)} custom-call(bf16[256,4096]{1,0:T(8,128)(2,1)} %feats_hbm.1, bf16[1024,256]{1,0:T(8,128)(2,1)} %adapter_hbm.1, bf16[1024,512]{1,0:T(8,128)(2,1)} %hist_hbm.1, bf16[512,256]{1,0:T(8,128)(2,1)} %wk_hbm.1, bf16[512,256]{1,0:T(8,128)(2,1)} %wv_hbm.1, s32[1,256]{1,0:T(1,128)} %bitcast.5, s32[1,64]{1,0:T(1,128)} %bitcast.7, ...), custom_call_target="tpu_custom_call" | custom-call | tf_op jit(solution)/shard_map/pallas_call | solution.py:429
  33.2 1.4 %copy.11 = bf16[64,256]{1,0:T(8,128)(2,1)} copy(bf16[64,256]{1,0:T(8,128)(2,1)} %shard_map.91) | data formatting | bytes 65536

commit v3 on v2

--- a/solution.py
+++ b/solution.py
@@ -8,7 +8,6 @@
 from jax.sharding import PartitionSpec as P
 
 HS = 64
-SUB = 2
 USERS = 256
 MESH = pl.DeviceIdType.MESH
 F32 = jnp.float32
@@ -26,6 +25,10 @@
             step(index)
     else:
         lax.fori_loop(low, high, lambda index, carry: (step(index), carry)[1], 0)
+
+
+def pieces(block):
+    return max(1, min(4, block // 64))
 
 
 def iota(shape, axis):
@@ -93,7 +96,13 @@
     sign = jnp.where(me < n // 2, 1, -1)
 
     def peer(d):
-        return lax.rem(me + sign * d + n, n)
+        if n > 8:
+            return lax.rem(me + sign * d + n, n)
+        found = 0
+        for at in range(n):
+            nearest = sorted(range(n), key=lambda p: abs(p - at))
+            found = jnp.where(me == at, nearest[d], found)
+        return found
 
     items, block = feats.shape[1], feats.shape[2]
     cols = ad.shape[2]
@@ -102,10 +111,11 @@
     events = hist.shape[0]
     entries = k_all.shape[0]
     owners = up(n, 8)
-    rows = block // (4 * SUB)
+    sub = pieces(block)
+    rows = block // (4 * sub)
 
     def share(a, b, k):
-        return pl.ds(pl.multiple_of(((a * 2 + b) * SUB + k) * rows, rows), rows)
+        return pl.ds(pl.multiple_of(((a * 2 + b) * sub + k) * rows, rows), rows)
 
     def remote(src, dst, send, recv, where):
         return pltpu.make_async_remote_copy(
@@ -113,7 +123,16 @@
         )
 
     barrier = pltpu.get_barrier_semaphore()
-    each(1, n, lambda d: pl.semaphore_signal(barrier, inc=1, device_id={"hist": peer(d)}, device_id_type=MESH))
+    has_left, has_right = me > 0, me < n - 1
+
+    @pl.when(has_right)
+    def _():
+        pl.semaphore_signal(barrier, inc=1, device_id={"hist": me + 1}, device_id_type=MESH)
+
+    @pl.when(has_left)
+    def _():
+        pl.semaphore_signal(barrier, inc=1, device_id={"hist": me - 1}, device_id_type=MESH)
+
     pl.semaphore_signal(barrier, inc=1, device_id={"rep": orep}, device_id_type=MESH)
     pl.semaphore_signal(barrier, inc=1, device_id={"groups": og}, device_id_type=MESH)
 
@@ -136,22 +155,22 @@
         )
 
     each(0, n, lambda s: feat_copy(s).start())
-    pl.semaphore_wait(barrier, n + 1)
+    pl.semaphore_wait(barrier, 2 + jnp.where(has_left, 1, 0) + jnp.where(has_right, 1, 0))
 
     def to_right(src, k, ref):
         return remote(
-            ref, ad.at[src, share(g, r, k)], right_send.at[src * SUB + k], z_recv.at[src * SUB + k], {"hist": me + 1}
+            ref, ad.at[src, share(g, r, k)], right_send.at[src * sub + k], z_recv.at[src * sub + k], {"hist": me + 1}
         )
 
     def to_left(src, k, ref):
         return remote(
-            ref, ad.at[src, share(g, r, k)], left_send.at[src * SUB + k], z_recv.at[src * SUB + k], {"hist": me - 1}
+            ref, ad.at[src, share(g, r, k)], left_send.at[src * sub + k], z_recv.at[src * sub + k], {"hist": me - 1}
         )
 
     def piece(src, a, b, k):
         return ad.at[src, share(a, b, k)]
 
-    for k in range(SUB):
+    for k in range(sub):
 
         @pl.when(me < n - 1)
         def _():
@@ -190,24 +209,23 @@
     event_counts = lax.dot_general(mine.astype(BF16), event_hot, NT, preferred_element_type=F32)
 
     meta_copy.wait_recv()
-    tab_all[me, 0:owners, 0:USERS] = counts + event_counts + meta_par[0:owners, 0:USERS]
-    tab_all[me, owners : owners + 8, 0:cands] = cand_user
+    summed = counts + event_counts + meta_par[0:owners, 0:USERS]
+    tab_all[me, 0:n, 0:USERS] = summed[0:n]
+    tab_all[me, n : n + 1, 0:cands] = cand_user[0:1]
 
     def t_copy(to):
         return remote(tab_all.at[me], tab_all.at[me], t_send.at[to], t_recv.at[me], {"hist": to})
 
-    each(1, n, lambda d: t_copy(peer(d)).start())
-
     def hop(src, a, b, k, sends, recvs, where):
         ref = piece(src, a, b, k)
-        return remote(ref, ref, sends.at[src * SUB + k], recvs.at[src * SUB + k], where)
+        return remote(ref, ref, sends.at[src * sub + k], recvs.at[src * sub + k], where)
 
     def spread(src, k):
         hop(src, g, r, k, y_send, y_recv, {"groups": og}).start()
         hop(src, g, r, k, p_send, p_recv, {"rep": orep}).start()
 
     def z_arrive(s):
-        for k in range(SUB):
+        for k in range(sub):
 
             @pl.when(me >= s)
             def _():
@@ -234,7 +252,7 @@
                 spread(src, k)
 
     def y_pass(src):
-        for k in range(SUB):
+        for k in range(sub):
             hop(src, og, r, k, y_send, y_recv, {"groups": og}).wait_recv()
             hop(src, og, r, k, pp_send, pp_recv, {"rep": orep}).start()
 
@@ -269,12 +287,44 @@
     own_block()
     each(3, n, lambda s: (z_arrive(s), y_arrive(s - 1)))
 
+    each(1, n, lambda d: t_copy(peer(n - d)).start())
+    y_arrive(n - 1)
+
+    def third(d):
+        src = peer(d)
+        for k in range(sub):
+            hop(src, g, orep, k, p_send, p_recv, {"rep": orep}).wait_recv()
+            hop(src, og, orep, k, pp_send, pp_recv, {"rep": orep}).wait_recv()
+        acc[...] += jnp.dot(feats[src], ad[src], preferred_element_type=F32)
+
+    each(1, n, third)
+
+    embedded = acc[...].astype(BF16)
+    own_q = jnp.dot(cand_hot, embedded, preferred_element_type=F32)
+    q_all[me] = own_q.astype(BF16)
+
+    def q_copy(to):
+        return remote(q_all.at[me], q_all.at[me], q_send.at[to], q_recv.at[me], {"hist": to})
+
+    each(1, n, lambda d: q_copy(peer(n - d)).start())
+    k_all[events : events + items, :] = embedded
+    v_all[events : events + items, :] = embedded
+    emb_copy = remote(
+        k_all.at[pl.ds(events, items)],
+        k_all.at[pl.ds(events + items, items)],
+        pair_send.at[1],
+        pair_recv.at[1],
+        {"rep": orep},
+    )
+    emb_copy.start()
+
     each(1, n, lambda d: remote(
         tab_all.at[peer(d)], tab_all.at[peer(d)], t_send.at[peer(d)], t_recv.at[peer(d)], {"hist": peer(d)}
     ).wait_recv())
     table = lax.fori_loop(
         0, n, lambda s, t: t + tab_all[s, 0:owners, 0:USERS], jnp.zeros((owners, USERS), F32)
     )
+    table = jnp.where(iota((owners, USERS), 0) < n, table, 0.0)
     high = jnp.floor(table * (1.0 / 256.0))
     split = jnp.concatenate([high, table - 256.0 * high], axis=0).astype(BF16)
 
@@ -294,42 +344,12 @@
         scale_of(hot(par_user, USERS).astype(BF16), hot(par_route, owners)), (8, items)
     )
 
-    y_arrive(n - 1)
-
-    def third(d):
-        src = peer(d)
-        for k in range(SUB):
-            hop(src, g, orep, k, p_send, p_recv, {"rep": orep}).wait_recv()
-            hop(src, og, orep, k, pp_send, pp_recv, {"rep": orep}).wait_recv()
-        acc[...] += jnp.dot(feats[src], ad[src], preferred_element_type=F32)
-
-    each(1, n, third)
-
-    embedded = acc[...].astype(BF16)
-    own_q = jnp.dot(cand_hot, embedded, preferred_element_type=F32)
-    q_all[me] = own_q.astype(BF16)
-
-    def q_copy(to):
-        return remote(q_all.at[me], q_all.at[me], q_send.at[to], q_recv.at[me], {"hist": to})
-
-    each(1, n, lambda d: q_copy(peer(n - d)).start())
-    k_all[events : events + items, :] = embedded
-    v_all[events : events + items, :] = embedded
-    emb_copy = remote(
-        k_all.at[pl.ds(events, items)],
-        k_all.at[pl.ds(events + items, items)],
-        pair_send.at[1],
-        pair_recv.at[1],
-        {"rep": orep},
-    )
-    emb_copy.start()
-
     head_of = iota((1, cols), 1) // HS
     eye = iota((cands, cands), 0) == iota((cands, cands), 1)
     width = math_block(entries)
 
     def user_column(p):
-        row = tab_all[p, owners : owners + 1, 0:cands]
+        row = tab_all[p, n : n + 1, 0:cands]
         return jnp.sum(jnp.where(eye, row, 0.0), axis=1, keepdims=True)
 
     def q_wait(p):
@@ -338,13 +358,12 @@
     def o_copy(to):
         return remote(part_out.at[to], part_in.at[me], o_send.at[to], o_recv.at[me], {"hist": to})
 
-    def chunk(pa, pb, opening):
+    def chunk(p, opening):
         if not opening:
-            q_wait(pa)
-        q_wait(pb)
-        q = jnp.concatenate([q_all[pa], q_all[pb]], axis=0) * jnp.asarray(0.5 * HS**-0.5, BF16)
-        ucol = jnp.concatenate([user_column(pa), user_column(pb)], axis=0)
-        count = 2 * cands
+            q_wait(p)
+        q = q_all[p] * jnp.asarray(0.5 * HS**-0.5, BF16)
+        ucol = user_column(p)
+        count = cands
         stacked = jnp.concatenate([jnp.where(head_of == h, q, jnp.zeros_like(q)) for h in range(heads)], axis=0)
         for start in range(0, entries, width):
             if opening and start + width > events + items and start <= events + items:
@@ -361,15 +380,13 @@
         for h in range(1, heads):
             total = jnp.where(head_of == h, mixed[h * count : (h + 1) * count], total)
         if opening:
-            own_part[...] = total[0:cands]
+            own_part[...] = total
         else:
-            part_out[pa] = total[0:cands].astype(BF16)
-            o_copy(pa).start()
-        part_out[pb] = total[cands:].astype(BF16)
-        o_copy(pb).start()
-
-    chunk(me, peer(1), True)
-    each(1, n // 2, lambda c: chunk(peer(2 * c), peer(2 * c + 1), False))
+            part_out[p] = total.astype(BF16)
+            o_copy(p).start()
+
+    chunk(me, True)
+    each(1, n, lambda d: chunk(peer(d), False))
 
     def collect(d):
         src = peer(d)
@@ -382,7 +399,7 @@
 
     def drain(d):
         p = peer(d)
-        for k in range(SUB):
+        for k in range(sub):
             hop(p, g, r, k, y_send, y_recv, {"groups": og}).wait_send()
             hop(p, g, r, k, p_send, p_recv, {"rep": orep}).wait_send()
             hop(p, og, r, k, pp_send, pp_recv, {"rep": orep}).wait_send()
@@ -395,13 +412,13 @@
     def drain_right(s):
         @pl.when((me >= s) & (me < n - 1))
         def _():
-            for k in range(SUB):
+            for k in range(sub):
                 to_right(me - s, k, piece(me - s, g, r, k)).wait_send()
 
     def drain_left(s):
         @pl.when((me + s < n) & (me > 0))
         def _():
-            for k in range(SUB):
+            for k in range(sub):
                 to_left(me + s, k, piece(me + s, g, r, k)).wait_send()
 
     each(0, n, lambda s: (drain_right(s), drain_left(s)))
@@ -421,6 +438,7 @@
     cands = cand_index.shape[0]
     heads = cols // HS
     owners = up(n, 8)
+    sub = pieces(block)
     wide = up(max(USERS, items, cands), 128)
     entries = events + 2 * items
     hbm = pl.BlockSpec(memory_space=pltpu.HBM)
@@ -450,14 +468,14 @@
             pltpu.VMEM((cands, cols), F32),
             pltpu.VMEM((owners + 8, wide), F32),
             pltpu.VMEM((owners + 8, wide), F32),
-            pltpu.VMEM((n, owners + 8, wide), F32),
+            pltpu.VMEM((n, up(n + 1, 8), wide), F32),
             pltpu.VMEM((8, entries), F32),
             pltpu.VMEM((8, entries), F32),
-            pltpu.VMEM((heads * 2 * cands, entries), BF16),
+            pltpu.VMEM((heads * cands, entries), BF16),
             dma((8,)),
             dma((n,)),
         ]
-        + [dma((n * SUB,))] * 9
+        + [dma((n * sub,))] * 9
         + [dma((n,))] * 6
         + [dma((2,)), dma((2,))],
         compiler_params=pltpu.CompilerParams(

time: 34.7 us -> 32.5 us (0.937)
  Pallas kernels: 33.2 us -> 30.9 us
    pallas_call x1, Pallas kernels: 33.2 us -> 30.9 us  [body(): pl.pallas_call(functools.partial(kernel, n), out_shape=jax.ShapeDtypeStru...]
where the time goes in v3:
time: 32.5 us; the launch traced here: 32.3 us
  Pallas kernels  30.9 us (95%)
  local copies, waits for them, and re-layouts  1.38 us (4%)
    pallas_call x1, Pallas kernels, body(): pl.pallas_call(functools.partial(kernel, n), out_shape=jax.ShapeDtypeStru...  30.9 us
    unnamed x1, local copies, waits for them, and re-layouts  1.38 us

profile of v3, /device:TPU:0, one launch (start us, length us, event | category | flops | bytes accessed | tf_op | source)
XLA Modules:
  0.0 32.3 jit_solution(17538517347459085970)
XLA Ops:
  0.0 30.9 %shard_map.91 = bf16[64,256]{1,0:T(8,128)(2,1)} custom-call(bf16[256,4096]{1,0:T(8,128)(2,1)} %feats_hbm.1, bf16[1024,256]{1,0:T(8,128)(2,1)} %adapter_hbm.1, bf16[1024,512]{1,0:T(8,128)(2,1)} %hist_hbm.1, bf16[512,256]{1,0:T(8,128)(2,1)} %wk_hbm.1, bf16[512,256]{1,0:T(8,128)(2,1)} %wv_hbm.1, s32[1,256]{1,0:T(1,128)} %bitcast.5, s32[1,64]{1,0:T(1,128)} %bitcast.7, ...), custom_call_target="tpu_custom_call" | custom-call | tf_op jit(solution)/shard_map/pallas_call | solution.py:447
  30.9 1.4 %copy.11 = bf16[64,256]{1,0:T(8,128)(2,1)} copy(bf16[64,256]{1,0:T(8,128)(2,1)} %shard_map.91) | data formatting | bytes 65536
